TPU v7x, 32 devices: a whole 2x2x4 slice. The times are simulated.
32 devices in a mesh: row: 4 (over y, core), col: 8 (over z, x).
Axes of the slice: x: 2, y: 2, z: 4, core: 2. Of those that a mesh axis runs over, the one named last changes fastest.
Arguments:
- kernel: float32 [4, 4, 256, 2, 8, 256], P(None, 'row', None, None, 'col'), may hold values from -40 to 40, as said below
Outputs:
- trailing: float32 [4, 4, 256, 2, 8, 256], P(None, 'row', None, None, 'col')
- panels: float32 [4, 4, 256, 3, 256], P(None, 'row')
Inputs may be any that keep to these rules, and one draw needn't show every extreme that they name: kernel is symmetric and positive definite with smallest eigenvalue at least 1.
All inputs are finite; a program needn't handle non-finite values.
Results may differ from a plain program's by a relative error of at most 0.0003.
Values sent between devices are 32-bit elements; how exact they have to be, the bound alone decides.
A program may use at most 128 MiB of HBM per device.

v0:
```python
import jax
import jax.numpy as jnp
from jax import lax
from jax.sharding import PartitionSpec as P

STEPS = 3


def broadcast(value, axis, source):
    kept = jnp.where(lax.axis_index(axis) == source, value, 0).astype(value.dtype)
    return lax.psum(kept, axis)


def shards(kernel):
    row_tiles, _, tile_size, col_tiles, _, _ = kernel.shape
    row_count = lax.axis_size("row")
    col_count = lax.axis_size("col")
    row_index = lax.axis_index("row")
    col_index = lax.axis_index("col")
    stride = col_count // row_count
    working = kernel.reshape(row_tiles, tile_size, col_tiles, tile_size)
    identity = jnp.eye(tile_size, dtype=jnp.float32)
    tile_rows = jnp.arange(row_tiles) * row_count + row_index
    tile_cols = jnp.arange(col_tiles) * col_count + col_index
    collected = []
    for panel_step in range(STEPS):
        local_row = panel_step // row_count
        local_col = panel_step // col_count
        column_slab = working[:, :, local_col, :]
        diagonal = broadcast(column_slab[local_row], "row", panel_step % row_count)
        factor = jnp.linalg.cholesky(diagonal)
        inverse = lax.linalg.triangular_solve(factor, identity, left_side=True, lower=True)
        panel = jnp.einsum("art,st->ars", column_slab, inverse, precision=lax.Precision.HIGHEST)
        panel = jnp.where((tile_rows >= panel_step)[:, None, None], panel, jnp.float32(0.0))
        my_panel = broadcast(panel, "col", panel_step % col_count)
        collected.append(my_panel)
        selected = lax.dynamic_index_in_dim(
            my_panel.reshape(col_tiles, stride, tile_size, tile_size),
            col_index // row_count,
            1,
            keepdims=False,
        )
        gathered = lax.all_gather(selected, "row", axis=0, tiled=True)
        col_panel = lax.dynamic_index_in_dim(
            gathered.reshape(row_count, col_tiles, tile_size, tile_size),
            col_index % row_count,
            0,
            keepdims=False,
        )
        row_terms = jnp.where((tile_rows > panel_step)[:, None, None], my_panel, jnp.float32(0.0))
        col_terms = jnp.where((tile_cols > panel_step)[:, None, None], col_panel, jnp.float32(0.0))
        correction = jnp.einsum(
            "art,cst->arcs", row_terms, col_terms, precision=lax.Precision.HIGHEST
        )
        keep_mask = (tile_rows > panel_step)[:, None, None, None] & (tile_cols > panel_step)[
            None, None, :, None
        ]
        working = jnp.where(keep_mask, working - correction, jnp.float32(0.0))
    trailing = working.reshape(kernel.shape)
    panels = jnp.stack(collected, axis=2).reshape(row_tiles, 1, tile_size, STEPS, tile_size)
    return (trailing, panels)


def solution(mesh):
    in_specs = (P(None, "row", None, None, "col", None),)
    out_specs = (P(None, "row", None, None, "col", None), P(None, "row", None, None, None))
    return jax.shard_map(shards, mesh=mesh, in_specs=in_specs, out_specs=out_specs, check_vma=False)
```

profile of v0, /device:TPU:0, one launch (start us, length us, event | category | flops | bytes accessed | tf_op | source)
XLA Modules:
  0.0 669.3 jit_solution(3093933253821480764)
XLA Ops:
  7.2 4.6 copy.23
  12.7 35.0 %all-reduce.8.cloned.1.call-done = f32[256,256]{0,1:T(8,128)} async-done(((f32[256,256]{0,1:T(8,128)}), f32[256,256]{0,1:T(8,128)}) %all-reduce.8.cloned.1.call-update) | async-done | bytes 262160 | tf_op jit(solution)/shard_map/psum | solution.py:11
  49.8 11.7 %cholesky.172 = f32[128,128]{1,0:T(8,128)S(1)} custom-call(f32[128,128]{1,0:T(8,128)S(1)} %cholesky.270), custom_call_target="Cholesky" | custom-call | tf_op jit(solution)/shard_map/jit(cholesky)/cholesky | solution.py:31
  61.5 9.8 %custom-call.15 = f32[1,128,128]{1,2,0:T(8,128)S(1)} custom-call(f32[1,128,128]{2,1,0:T(8,128)S(1)} %get-tuple-element.72), custom_call_target="InvertDiagBlocksLowerTriangular" | custom-call | tf_op jit(solution)/shard_map/jit(cholesky)/cholesky | solution.py:31
  71.9 11.7 %cholesky.189 = f32[128,128]{1,0:T(8,128)S(1)} custom-call(f32[128,128]{1,0:T(8,128)S(1)} %convolution_subtract_fusion.5), custom_call_target="Cholesky" | custom-call | tf_op jit(solution)/shard_map/jit(cholesky)/cholesky | solution.py:31
  85.8 4.6 while.6
  90.4 19.7 %custom-call.16 = f32[2,128,128]{1,2,0:T(8,128)S(1)} custom-call(f32[2,128,128]{2,1,0:T(8,128)S(1)} %get-tuple-element.24), custom_call_target="InvertDiagBlocksLowerTriangular" | custom-call | tf_op jit(solution)/shard_map/triangular_solve/custom-call.0 | solution.py:32
  113.1 78.4 %all-reduce.10.cloned.1.call-done = f32[4,256,256]{1,2,0:T(8,128)} async-done(((f32[4,256,256]{1,2,0:T(8,128)}), f32[4,256,256]{1,2,0:T(8,128)}) %all-reduce.10.cloned.1.call-update) | async-done | bytes 1048592 | tf_op jit(solution)/shard_map/psum | solution.py:11
  195.8 22.1 %all-gather.7.cloned.1.call-done = f32[8,1,256,256]{3,2,1,0:T(8,128)} async-done(((f32[2,1,256,256]{3,2,1,0:T(8,128)}), f32[8,1,256,256]{3,2,1,0:T(8,128)}) %all-gather.7.cloned.1.call-update) | async-done | bytes 2097168 | tf_op jit(solution)/shard_map/all_gather | solution.py:43
  217.9 3.2 subtract_select_fusion.1
  223.4 32.2 %all-reduce.12.cloned.1.call-done = f32[256,256]{0,1:T(8,128)} async-done(((f32[256,256]{0,1:T(8,128)}), f32[256,256]{0,1:T(8,128)}) %all-reduce.12.cloned.1.call-update) | async-done | bytes 262160 | tf_op jit(solution)/shard_map/psum | solution.py:11
  258.4 11.7 %cholesky.206 = f32[128,128]{1,0:T(8,128)S(1)} custom-call(f32[128,128]{1,0:T(8,128)S(1)} %cholesky.273), custom_call_target="Cholesky" | custom-call | tf_op jit(solution)/shard_map/jit(cholesky)/cholesky | solution.py:31
  270.8 10.4 %custom-call.17 = f32[1,128,128]{1,2,0:T(8,128)} custom-call(f32[1,128,128]{2,1,0:T(8,128)S(1)} %get-tuple-element.68), custom_call_target="InvertDiagBlocksLowerTriangular" | custom-call | tf_op jit(solution)/shard_map/jit(cholesky)/cholesky | solution.py:31
  284.7 11.7 %cholesky.223 = f32[128,128]{1,0:T(8,128)S(1)} custom-call(f32[128,128]{1,0:T(8,128)S(1)} %convolution_subtract_fusion.4), custom_call_target="Cholesky" | custom-call | tf_op jit(solution)/shard_map/jit(cholesky)/cholesky | solution.py:31
  299.8 6.0 while.7
  306.5 20.5 %custom-call.18 = f32[2,128,128]{1,2,0:T(8,128)S(1)} custom-call(f32[2,128,128]{2,1,0:T(8,128)} %copy-done.7), custom_call_target="InvertDiagBlocksLowerTriangular" | custom-call | tf_op jit(solution)/shard_map/triangular_solve/custom-call.0 | solution.py:32
  330.9 78.4 %all-reduce.14.cloned.1.call-done = f32[4,256,256]{1,2,0:T(8,128)} async-done(((f32[4,256,256]{1,2,0:T(8,128)}), f32[4,256,256]{1,2,0:T(8,128)}) %all-reduce.14.cloned.1.call-update) | async-done | bytes 1048592 | tf_op jit(solution)/shard_map/psum | solution.py:11
  411.6 22.2 %all-gather.9.cloned.1.call-done = f32[8,1,256,256]{3,2,1,0:T(8,128)} async-done(((f32[2,1,256,256]{3,2,1,0:T(8,128)}), f32[8,1,256,256]{3,2,1,0:T(8,128)}) %all-gather.9.cloned.1.call-update) | async-done | bytes 2097168 | tf_op jit(solution)/shard_map/all_gather | solution.py:43
  433.8 4.2 subtract_select_fusion
  439.0 32.1 %all-reduce.16.cloned.1.call-done = f32[256,256]{0,1:T(8,128)} async-done(((f32[256,256]{0,1:T(8,128)}), f32[256,256]{0,1:T(8,128)}) %all-reduce.16.cloned.1.call-update) | async-done | bytes 262160 | tf_op jit(solution)/shard_map/psum | solution.py:11
  474.7 11.7 %cholesky.240 = f32[128,128]{1,0:T(8,128)S(1)} custom-call(f32[128,128]{1,0:T(8,128)S(1)} %cholesky.276), custom_call_target="Cholesky" | custom-call | tf_op jit(solution)/shard_map/jit(cholesky)/cholesky | solution.py:31
  487.1 10.4 %custom-call.19 = f32[1,128,128]{1,2,0:T(8,128)} custom-call(f32[1,128,128]{2,1,0:T(8,128)S(1)} %get-tuple-element.64), custom_call_target="InvertDiagBlocksLowerTriangular" | custom-call | tf_op jit(solution)/shard_map/jit(cholesky)/cholesky | solution.py:31
  501.1 11.7 %cholesky.257 = f32[128,128]{1,0:T(8,128)S(1)} custom-call(f32[128,128]{1,0:T(8,128)S(1)} %convolution_subtract_fusion.3), custom_call_target="Cholesky" | custom-call | tf_op jit(solution)/shard_map/jit(cholesky)/cholesky | solution.py:31
  516.1 6.0 while.8
  517.0 2.3 bitcast_dynamic-update-slice_fusion.8
  522.7 20.5 %custom-call.20 = f32[2,128,128]{1,2,0:T(8,128)S(1)} custom-call(f32[2,128,128]{2,1,0:T(8,128)} %copy-done.6), custom_call_target="InvertDiagBlocksLowerTriangular" | custom-call | tf_op jit(solution)/shard_map/triangular_solve/custom-call.0 | solution.py:32
  547.1 78.4 %all-reduce.18.cloned.1.call-done = f32[4,256,256]{1,2,0:T(8,128)} async-done(((f32[4,256,256]{1,2,0:T(8,128)}), f32[4,256,256]{1,2,0:T(8,128)}) %all-reduce.18.cloned.1.call-update) | async-done | bytes 1048592 | tf_op jit(solution)/shard_map/psum | solution.py:11
  629.5 3.4 maximum_bitcast_fusion
  632.9 3.6 copy.42
  636.6 15.2 %all-gather.11.cloned.1.call-done = f32[8,1,256,256]{3,2,1,0:T(8,128)} async-done(((f32[2,1,256,256]{3,2,1,0:T(8,128)}), f32[8,1,256,256]{3,2,1,0:T(8,128)}) %all-gather.11.cloned.1.call-update) | async-done | bytes 2097168 | tf_op jit(solution)/shard_map/all_gather | solution.py:43
  651.7 4.5 select_bitcast_fusion
  656.3 6.0 copy.41
  (122 shorter events, 62.0 us)
Async XLA Ops:
  7.2 40.5 %all-reduce.8.cloned.1.call-start = ((), (), s32[]{:S(2)}) async-start(), calls=%async_computation | async-start | bytes 524288 | tf_op jit(solution)/shard_map/psum | solution.py:11
  12.5 179.0 %all-reduce.10.cloned.1.call-start = ((), (), s32[]{:S(2)}) async-start(), calls=%async_computation.1 | async-start | bytes 2097152 | tf_op jit(solution)/shard_map/psum | solution.py:11
  113.1 104.9 %all-gather.7.cloned.1.call-start = ((), (), s32[]{:S(2)}) async-start(), calls=%async_computation.6 | async-start | bytes 2621440 | tf_op jit(solution)/shard_map/all_gather | solution.py:43
  191.6 26.3 %copy-start.2 = (f32[4,256,256]{1,2,0:T(8,128)S(1)}, f32[4,256,256]{1,2,0:T(8,128)}, u32[]{:S(2)}) copy-start(f32[4,256,256]{1,2,0:T(8,128)} %all-reduce.10.cloned.1.call-done) | copy-start | bytes 3145732
  195.6 60.0 %all-reduce.12.cloned.1.call-start = ((), (), s32[]{:S(2)}) async-start(), calls=%async_computation.2 | async-start | bytes 524288 | tf_op jit(solution)/shard_map/psum | solution.py:11
  221.1 1.3 copy-start
  223.2 186.2 %all-reduce.14.cloned.1.call-start = ((), (), s32[]{:S(2)}) async-start(), calls=%async_computation.3 | async-start | bytes 2097152 | tf_op jit(solution)/shard_map/psum | solution.py:11
  257.7 0.7 copy-start.4
  258.4 70.4 %copy-start.1 = (f32[4,256,2,256]{1,3,2,0:T(8,128)S(1)}, f32[4,256,2,256]{1,3,2,0:T(8,128)}, u32[]{:S(2)}) copy-start(f32[4,256,2,256]{1,3,2,0:T(8,128)} %copy-done) | copy-start | bytes 6291460
  305.9 0.6 copy-start.7
  330.8 102.9 %all-gather.9.cloned.1.call-start = ((), (), s32[]{:S(2)}) async-start(), calls=%async_computation.7 | async-start | bytes 2621440 | tf_op jit(solution)/shard_map/all_gather | solution.py:43
  411.4 59.7 %all-reduce.16.cloned.1.call-start = ((), (), s32[]{:S(2)}) async-start(), calls=%async_computation.4 | async-start | bytes 524288 | tf_op jit(solution)/shard_map/psum | solution.py:11
  438.7 186.8 %all-reduce.18.cloned.1.call-start = ((), (), s32[]{:S(2)}) async-start(), calls=%async_computation.5 | async-start | bytes 2097152 | tf_op jit(solution)/shard_map/psum | solution.py:11
  474.0 0.7 copy-start.5
  522.1 0.7 copy-start.6
  547.1 104.7 %all-gather.11.cloned.1.call-start = ((), (), s32[]{:S(2)}) async-start(), calls=%async_computation.8 | async-start | bytes 2621440 | tf_op jit(solution)/shard_map/all_gather | solution.py:43
  632.9 18.8 %copy-start.3 = (f32[4,256,256]{1,2,0:T(8,128)S(1)}, f32[4,256,256]{1,2,0:T(8,128)}, u32[]{:S(2)}) copy-start(f32[4,256,256]{1,2,0:T(8,128)} %all-reduce.18.cloned.1.call-done) | copy-start | bytes 3145732
Sparse Core Ops, SparseCore 0:
  12.7 34.9 all-reduce.7
  113.2 78.3 all-reduce.9
  195.7 22.1 all-gather.6
  223.3 32.2 all-reduce.11
  331.0 78.3 all-reduce.13
  411.6 22.1 all-gather.8
  438.8 32.2 all-reduce.15
  547.2 78.2 all-reduce.17
  629.5 22.1 all-gather.10
where the time goes:
time: 678 us; the launch traced here: 669 us
  waiting for transfers between devices  394 us (58%)
  other arithmetic  177 us (26%)
  local copies, waits for them, and re-layouts  49.2 us (7%)
  matrix products  28.4 us (4%)
  between operations  18.7 us (3%)
    psum x6, waiting for transfers between devices, broadcast(): return lax.psum(kept, axis)  335 us
    another operation x20, other arithmetic, shards(): factor = jnp.linalg.cholesky(diagonal)  106 us
    another operation x7, other arithmetic, shards(): lax.linalg.triangular_solve(factor, identity, left_side=True, lower=True)  62.2 us
    all_gather x3, waiting for transfers between devices, shards(): gathered = lax.all_gather(selected, 'row', axis=0, tiled=True)  59.5 us
    unnamed x22, local copies, waits for them, and re-layouts  23.3 us
    another operation x22, local copies, waits for them, and re-layouts, shards(): lax.linalg.triangular_solve(factor, identity, left_side=True, lower=True)  15.6 us
  transfers between devices with their start and end apart: 9, of which 9 were waited for; matrix products, arithmetic and copies ran while one was open for 1% of the time, Pallas kernels for 0%

commit v1 on v0

--- a/solution.py
+++ b/solution.py
@@ -2,13 +2,20 @@
 import jax.numpy as jnp
 from jax import lax
 from jax.sharding import PartitionSpec as P
+from jax.lax import all_gather
 
 STEPS = 3
 
 
+def produce_the_edge(shard_axis, incoming_x):
+    fresh = all_gather(incoming_x, shard_axis)
+    long_array = jnp.sum(fresh, axis=0)
+    return long_array
+
+
 def broadcast(value, axis, source):
     kept = jnp.where(lax.axis_index(axis) == source, value, 0).astype(value.dtype)
-    return lax.psum(kept, axis)
+    return produce_the_edge(axis, kept)
 
 
 def shards(kernel):

time: 678 us -> 768 us (1.13)
  waiting for transfers between devices: 394 us -> 485 us
  other arithmetic: 177 us -> 192 us
  local copies, waits for them, and re-layouts: 49.2 us -> 36.3 us
    all_gather x0 -> x6, waiting for transfers between devices: none -> 426 us  [produce_the_edge(): fresh = all_gather(incoming_x, shard_axis)]
    psum x6 -> x0, waiting for transfers between devices: 335 us -> none  [broadcast(): return lax.psum(kept, axis)]
    reduce_sum x0 -> x6, other arithmetic: none -> 18.5 us  [produce_the_edge(): long_array = jnp.sum(fresh, axis=0)]
    unnamed x22 -> x19, local copies, waits for them, and re-layouts: 23.3 us -> 11.3 us
where the time goes in v1:
time: 768 us; the launch traced here: 759 us
  waiting for transfers between devices  485 us (63%)
  other arithmetic  192 us (25%)
  local copies, waits for them, and re-layouts  36.3 us (5%)
  matrix products  26.3 us (3%)
  between operations  18.4 us (2%)
    all_gather x6, waiting for transfers between devices, produce_the_edge(): fresh = all_gather(incoming_x, shard_axis)  426 us
    another operation x20, other arithmetic, shards(): factor = jnp.linalg.cholesky(diagonal)  105 us
    another operation x7, other arithmetic, shards(): lax.linalg.triangular_solve(factor, identity, left_side=True, lower=True)  62.2 us
    all_gather x3, waiting for transfers between devices, shards(): gathered = lax.all_gather(selected, 'row', axis=0, tiled=True)  58.3 us
    reduce_sum x6, other arithmetic, produce_the_edge(): long_array = jnp.sum(fresh, axis=0)  18.5 us
    another operation x22, local copies, waits for them, and re-layouts, shards(): lax.linalg.triangular_solve(factor, identity, left_side=True, lower=True)  15.7 us
  transfers between devices with their start and end apart: 9, of which 9 were waited for; matrix products, arithmetic and copies ran while one was open for 1% of the time, Pallas kernels for 0%

profile of v1, /device:TPU:0, one launch (start us, length us, event | category | flops | bytes accessed | tf_op | source)
XLA Modules:
  0.0 759.3 jit_solution(15331327212120473767)
XLA Ops:
  9.9 19.7 %all-gather.19.cloned.1.call-done = f32[4,256,1,256]{3,1,2,0:T(8,128)} async-done(((f32[1,256,1,256]{3,1,2,0:T(8,128)}), f32[4,256,1,256]{3,1,2,0:T(8,128)}) %all-gather.19.cloned.1.call-update) | async-done | bytes 1048592 | tf_op jit(solution)/shard_map/all_gather | solution.py:11
  31.1 11.7 %cholesky.172 = f32[128,128]{1,0:T(8,128)S(1)} custom-call(f32[128,128]{1,0:T(8,128)S(1)} %cholesky.270), custom_call_target="Cholesky" | custom-call | tf_op jit(solution)/shard_map/jit(cholesky)/cholesky | solution.py:38
  42.8 9.8 %custom-call.15 = f32[1,128,128]{1,2,0:T(8,128)S(1)} custom-call(f32[1,128,128]{2,1,0:T(8,128)S(1)} %get-tuple-element.72), custom_call_target="InvertDiagBlocksLowerTriangular" | custom-call | tf_op jit(solution)/shard_map/jit(cholesky)/cholesky | solution.py:38
  53.2 11.7 %cholesky.189 = f32[128,128]{1,0:T(8,128)S(1)} custom-call(f32[128,128]{1,0:T(8,128)S(1)} %convolution_subtract_fusion.5), custom_call_target="Cholesky" | custom-call | tf_op jit(solution)/shard_map/jit(cholesky)/cholesky | solution.py:38
  67.1 4.3 while.6
  71.4 19.7 %custom-call.16 = f32[2,128,128]{1,2,0:T(8,128)S(1)} custom-call(f32[2,128,128]{2,1,0:T(8,128)S(1)} %get-tuple-element.24), custom_call_target="InvertDiagBlocksLowerTriangular" | custom-call | tf_op jit(solution)/shard_map/triangular_solve/custom-call.0 | solution.py:39
  94.4 124.6 %all-gather.21.cloned.1.call-done = f32[32,256,256]{2,1,0:T(8,128)} async-done(((f32[4,256,256]{2,1,0:T(8,128)}), f32[32,256,256]{2,1,0:T(8,128)}) %all-gather.21.cloned.1.call-update) | async-done | bytes 8388624 | tf_op jit(solution)/shard_map/all_gather | solution.py:11
  219.0 4.1 reduce_sum.55
  224.6 20.7 %all-gather.23.cloned.1.call-done = f32[8,1,256,256]{3,2,1,0:T(8,128)} async-done(((f32[2,1,256,256]{3,2,1,0:T(8,128)}), f32[8,1,256,256]{3,2,1,0:T(8,128)}) %all-gather.23.cloned.1.call-update) | async-done | bytes 2097168 | tf_op jit(solution)/shard_map/all_gather | solution.py:50
  245.4 3.8 subtract_select_fusion.1
  250.2 16.6 %all-gather.25.cloned.1.call-done = f32[4,256,1,256]{3,1,2,0:T(8,128)} async-done(((f32[1,256,1,256]{3,1,2,0:T(8,128)}), f32[4,256,1,256]{3,1,2,0:T(8,128)}) %all-gather.25.cloned.1.call-update) | async-done | bytes 1048592 | tf_op jit(solution)/shard_map/all_gather | solution.py:11
  272.4 11.7 %cholesky.206 = f32[128,128]{1,0:T(8,128)S(1)} custom-call(f32[128,128]{1,0:T(8,128)S(1)} %cholesky.273), custom_call_target="Cholesky" | custom-call | tf_op jit(solution)/shard_map/jit(cholesky)/cholesky | solution.py:38
  284.8 9.8 %custom-call.17 = f32[1,128,128]{1,2,0:T(8,128)S(1)} custom-call(f32[1,128,128]{2,1,0:T(8,128)S(1)} %get-tuple-element.68), custom_call_target="InvertDiagBlocksLowerTriangular" | custom-call | tf_op jit(solution)/shard_map/jit(cholesky)/cholesky | solution.py:38
  297.4 11.7 %cholesky.223 = f32[128,128]{1,0:T(8,128)S(1)} custom-call(f32[128,128]{1,0:T(8,128)S(1)} %convolution_subtract_fusion.4), custom_call_target="Cholesky" | custom-call | tf_op jit(solution)/shard_map/jit(cholesky)/cholesky | solution.py:38
  313.1 6.1 while.7
  314.1 2.2 bitcast_dynamic-update-slice_fusion.7
  319.9 20.5 %custom-call.18 = f32[2,128,128]{1,2,0:T(8,128)S(1)} custom-call(f32[2,128,128]{2,1,0:T(8,128)} %copy-done.5), custom_call_target="InvertDiagBlocksLowerTriangular" | custom-call | tf_op jit(solution)/shard_map/triangular_solve/custom-call.0 | solution.py:39
  344.2 124.6 %all-gather.27.cloned.1.call-done = f32[32,256,256]{2,1,0:T(8,128)} async-done(((f32[4,256,256]{2,1,0:T(8,128)}), f32[32,256,256]{2,1,0:T(8,128)}) %all-gather.27.cloned.1.call-update) | async-done | bytes 8388624 | tf_op jit(solution)/shard_map/all_gather | solution.py:11
  468.8 4.1 reduce_sum.57
  473.9 20.7 %all-gather.29.cloned.1.call-done = f32[8,1,256,256]{3,2,1,0:T(8,128)} async-done(((f32[2,1,256,256]{3,2,1,0:T(8,128)}), f32[8,1,256,256]{3,2,1,0:T(8,128)}) %all-gather.29.cloned.1.call-update) | async-done | bytes 2097168 | tf_op jit(solution)/shard_map/all_gather | solution.py:50
  494.7 4.1 subtract_select_fusion
  500.0 16.3 %all-gather.31.cloned.1.call-done = f32[4,256,1,256]{3,1,2,0:T(8,128)} async-done(((f32[1,256,1,256]{3,1,2,0:T(8,128)}), f32[4,256,1,256]{3,1,2,0:T(8,128)}) %all-gather.31.cloned.1.call-update) | async-done | bytes 1048592 | tf_op jit(solution)/shard_map/all_gather | solution.py:11
  521.9 11.7 %cholesky.240 = f32[128,128]{1,0:T(8,128)S(1)} custom-call(f32[128,128]{1,0:T(8,128)S(1)} %cholesky.276), custom_call_target="Cholesky" | custom-call | tf_op jit(solution)/shard_map/jit(cholesky)/cholesky | solution.py:38
  534.4 9.8 %custom-call.19 = f32[1,128,128]{1,2,0:T(8,128)S(1)} custom-call(f32[1,128,128]{2,1,0:T(8,128)S(1)} %get-tuple-element.64), custom_call_target="InvertDiagBlocksLowerTriangular" | custom-call | tf_op jit(solution)/shard_map/jit(cholesky)/cholesky | solution.py:38
  547.0 11.7 %cholesky.257 = f32[128,128]{1,0:T(8,128)S(1)} custom-call(f32[128,128]{1,0:T(8,128)S(1)} %convolution_subtract_fusion.3), custom_call_target="Cholesky" | custom-call | tf_op jit(solution)/shard_map/jit(cholesky)/cholesky | solution.py:38
  562.7 6.0 while.8
  569.3 20.5 %custom-call.20 = f32[2,128,128]{1,2,0:T(8,128)S(1)} custom-call(f32[2,128,128]{2,1,0:T(8,128)} %copy-done.6), custom_call_target="InvertDiagBlocksLowerTriangular" | custom-call | tf_op jit(solution)/shard_map/triangular_solve/custom-call.0 | solution.py:39
  593.6 124.6 %all-gather.33.cloned.1.call-done = f32[32,256,256]{2,1,0:T(8,128)} async-done(((f32[4,256,256]{2,1,0:T(8,128)}), f32[32,256,256]{2,1,0:T(8,128)}) %all-gather.33.cloned.1.call-update) | async-done | bytes 8388624 | tf_op jit(solution)/shard_map/all_gather | solution.py:11
  718.2 5.0 reduce_sum.59
  729.2 16.8 %all-gather.35.cloned.1.call-done = f32[8,1,256,256]{3,2,1,0:T(8,128)} async-done(((f32[2,1,256,256]{3,2,1,0:T(8,128)}), f32[8,1,256,256]{3,2,1,0:T(8,128)}) %all-gather.35.cloned.1.call-update) | async-done | bytes 2097168 | tf_op jit(solution)/shard_map/all_gather | solution.py:50
  746.1 3.1 select_bitcast_fusion
  749.1 3.5 copy.30
  (126 shorter events, 65.5 us)
Async XLA Ops:
  7.2 22.4 %all-gather.19.cloned.1.call-start = ((), (), s32[]{:S(2)}) async-start(), calls=%async_computation | async-start | bytes 1310720 | tf_op jit(solution)/shard_map/all_gather | solution.py:11
  9.8 209.2 %all-gather.21.cloned.1.call-start = ((), (), s32[]{:S(2)}) async-start(), calls=%async_computation.1 | async-start | bytes 9437184 | tf_op jit(solution)/shard_map/all_gather | solution.py:11
  94.4 151.0 %all-gather.23.cloned.1.call-start = ((), (), s32[]{:S(2)}) async-start(), calls=%async_computation.2 | async-start | bytes 2621440 | tf_op jit(solution)/shard_map/all_gather | solution.py:50
  224.5 42.3 %all-gather.25.cloned.1.call-start = ((), (), s32[]{:S(2)}) async-start(), calls=%async_computation.3 | async-start | bytes 1310720 | tf_op jit(solution)/shard_map/all_gather | solution.py:11
  249.1 93.0 %copy-start = (f32[4,256,2,256]{3,1,0,2:T(8,128)}, f32[4,256,2,256]{3,1,0,2:T(8,128)S(1)}, u32[]{:S(2)}) copy-start(f32[4,256,2,256]{3,1,0,2:T(8,128)S(1)} %subtract_select_fusion.1) | copy-start | bytes 6291460
  249.9 218.8 %all-gather.27.cloned.1.call-start = ((), (), s32[]{:S(2)}) async-start(), calls=%async_computation.4 | async-start | bytes 9437184 | tf_op jit(solution)/shard_map/all_gather | solution.py:11
  271.7 0.7 copy-start.3
  319.2 0.6 copy-start.5
  344.1 150.6 %all-gather.29.cloned.1.call-start = ((), (), s32[]{:S(2)}) async-start(), calls=%async_computation.5 | async-start | bytes 2621440 | tf_op jit(solution)/shard_map/all_gather | solution.py:50
  472.8 21.9 %copy-start.1 = (f32[4,256,256]{2,1,0:T(8,128)}, f32[4,256,256]{2,1,0:T(8,128)S(1)}, u32[]{:S(2)}) copy-start(f32[4,256,256]{2,1,0:T(8,128)S(1)} %reduce_sum.57) | copy-start | bytes 3145732
  473.8 42.6 %all-gather.31.cloned.1.call-start = ((), (), s32[]{:S(2)}) async-start(), calls=%async_computation.6 | async-start | bytes 1310720 | tf_op jit(solution)/shard_map/all_gather | solution.py:11
  499.5 218.7 %all-gather.33.cloned.1.call-start = ((), (), s32[]{:S(2)}) async-start(), calls=%async_computation.7 | async-start | bytes 9437184 | tf_op jit(solution)/shard_map/all_gather | solution.py:11
  521.2 0.7 copy-start.4
  568.7 0.6 copy-start.6
  593.6 152.5 %all-gather.35.cloned.1.call-start = ((), (), s32[]{:S(2)}) async-start(), calls=%async_computation.8 | async-start | bytes 2621440 | tf_op jit(solution)/shard_map/all_gather | solution.py:50
  727.2 18.9 %copy-start.2 = (f32[4,256,256]{2,1,0:T(8,128)S(1)}, f32[4,256,256]{2,1,0:T(8,128)}, u32[]{:S(2)}) copy-start(f32[4,256,256]{2,1,0:T(8,128)} %reduce_sum.59) | copy-start | bytes 3145732
Sparse Core Ops, SparseCore 0:
  10.1 19.4 all-gather.18
  94.5 124.4 all-gather.20
  224.6 20.7 all-gather.22
  250.1 16.6 all-gather.24
  344.2 124.4 all-gather.26
  473.9 20.7 all-gather.28
  499.6 16.6 all-gather.30
  593.7 124.4 all-gather.32
  725.3 20.7 all-gather.34
